TPU v7x, 256 devices: a whole 4x4x8 slice. The times are simulated.
256 devices in a mesh: curve: 128 (over y_lo, z, x, core), dp: 2 (over y_hi).
Axes of the slice: x: 4, y: 4 (y_hi: 2, y_lo: 2; y = y_hi * 2 + y_lo), z: 8, core: 2. Of those that a mesh axis runs over, the one named last changes fastest.
Arguments:
- points: bfloat16 [2, 65536, 512], P('dp', 'curve'), may hold values from -24 to 24
- grad_out: bfloat16 [2, 65536, 512], P('dp', 'curve'), may hold values from -6 to 6
- dest_dev: int32 [2, 65536], P('dp', 'curve'), may hold values from 0 to 127, as said below
- dest_row: int32 [2, 65536], P('dp', 'curve'), may hold values from 0 to 511
- w_qkv: bfloat16 [512, 1536], replicated, may hold values from -1 to 1
- w_out: bfloat16 [512, 512], replicated, may hold values from -0.25 to 0.25
Outputs:
- grad_points: bfloat16 [2, 65536, 512], P('dp', 'curve')
- grad_w_qkv: float32 [512, 1536], replicated
- grad_w_out: float32 [512, 512], replicated
Inputs may be any that keep to these rules, and one draw needn't show every extreme that they name: `dest_dev`: together with dest_row it maps each group's scan points one to one onto the 65536 curve positions: every curve device of a group receives exactly 512 points, at most 8 of them from one scan device, and in every draw some scan device sends exactly 8 points to some curve device.
All inputs are finite; a program needn't handle non-finite values.
Results may differ from a plain program's by a relative error of at most 0.011.
The roundings to bfloat16 on the way count: a program that leaves them out, or rounds other values in their place, can miss the bound.
Values may be sent and summed in bfloat16 or wider, within the bound.
A program may use at most 64 MiB of HBM per device.

v0:
```python
import functools
import math

import jax
import jax.numpy as jnp
from jax import lax
from jax.experimental import pallas as pl
from jax.experimental.pallas import tpu as pltpu
from jax.sharding import PartitionSpec as P

HEADS = 8
PATCH = 512
CAP = 8
MESH = pl.DeviceIdType.MESH
BF16 = jnp.bfloat16
F32 = jnp.float32
I32 = jnp.int32
VMEM_SPEC = pl.BlockSpec(memory_space=pltpu.VMEM)
ANY_SPEC = pl.BlockSpec(memory_space=pl.ANY)


def dot_nn(a, b):
    return lax.dot_general(a, b, (((1,), (0,)), ((), ())), preferred_element_type=F32)


def dot_nt(a, b):
    return lax.dot_general(a, b, (((1,), (1,)), ((), ())), preferred_element_type=F32)


def iota(shape, dim):
    return lax.broadcasted_iota(I32, shape, dim)


def onehot(mask):
    return jnp.where(mask, 1.0, 0.0).astype(BF16)


def pack_kernel(dev_ref, row_ref, points_ref, grads_ref, send_ref, meta_ref, slot_ref):
    n_dev = send_ref.shape[0]
    rows = points_ref.shape[0]
    dev = dev_ref[...]
    mask = iota((n_dev, rows), 0) == dev
    hot = onehot(mask)
    upper = onehot(iota((rows, rows), 0) <= iota((rows, rows), 1))
    running = dot_nn(hot, upper)
    rank = jnp.sum(jnp.where(mask, running, 0.0), axis=0, keepdims=True).astype(I32) - 1
    slot_ref[...] = dev * CAP + rank
    coded = row_ref[...] + 1
    at_rank = iota((128, rows), 0) == rank
    high = jnp.where(at_rank, (coded >> 8).astype(F32), 0.0).astype(BF16)
    low = jnp.where(at_rank, (coded & 255).astype(F32), 0.0).astype(BF16)
    meta_ref[...] = dot_nt(hot, high) * 256.0 + dot_nt(hot, low)
    slot = dev * (2 * CAP) + rank
    points = points_ref[...]
    grads = grads_ref[...]
    chunk = 16

    def body(step, carry):
        base = step * (chunk * 2 * CAP)
        ids = iota((chunk * 2 * CAP, rows), 0) + base
        block = dot_nn(onehot(ids == slot), points) + dot_nn(onehot(ids == slot + CAP), grads)
        send_ref[pl.ds(step * chunk, chunk)] = block.astype(BF16).reshape(chunk, 2 * CAP, -1)
        return carry

    lax.fori_loop(0, n_dev // chunk, body, 0)


def pack(dev, row, points, grads, n_dev):
    rows, width = points.shape
    return pl.pallas_call(
        pack_kernel,
        out_shape=(
            jax.ShapeDtypeStruct((n_dev, 2 * CAP, width), BF16),
            jax.ShapeDtypeStruct((n_dev, 128), F32),
            jax.ShapeDtypeStruct((1, rows), I32),
        ),
        in_specs=[VMEM_SPEC] * 4,
        out_specs=(VMEM_SPEC,) * 3,
        name="pack",
    )(dev, row, points, grads)


def exchange_kernel(count, *refs):
    sends, gets = refs[:count], refs[count : 2 * count]
    send_sem, recv_sem, local_sem = refs[2 * count :]
    n_dev = sends[0].shape[0]
    me = lax.axis_index("curve")
    barrier = pltpu.get_barrier_semaphore()

    def greet(k, carry):
        peer = lax.rem(me + k, n_dev)
        pl.semaphore_signal(barrier, inc=1, device_id={"curve": peer}, device_id_type=MESH)
        return carry

    lax.fori_loop(1, n_dev, greet, 0)
    pl.semaphore_wait(barrier, n_dev - 1)

    def start(k, carry):
        peer = lax.rem(me + k, n_dev)
        for i in range(count):
            pltpu.make_async_remote_copy(
                src_ref=sends[i].at[peer],
                dst_ref=gets[i].at[me],
                send_sem=send_sem.at[i],
                recv_sem=recv_sem.at[i],
                device_id={"curve": peer},
                device_id_type=MESH,
            ).start()
        return carry

    lax.fori_loop(1, n_dev, start, 0)
    own = [
        pltpu.make_async_copy(sends[i].at[me], gets[i].at[me], local_sem.at[i])
        for i in range(count)
    ]
    for copy in own:
        copy.start()
    for copy in own:
        copy.wait()
    for i in range(count):
        others = pl.ds(0, n_dev - 1)
        pltpu.make_async_copy(sends[i].at[others], sends[i].at[others], send_sem.at[i]).wait()
        pltpu.make_async_copy(gets[i].at[others], gets[i].at[others], recv_sem.at[i]).wait()


def exchange(blocks, collective_id, name):
    count = len(blocks)
    return pl.pallas_call(
        functools.partial(exchange_kernel, count),
        out_shape=tuple(jax.ShapeDtypeStruct(b.shape, b.dtype) for b in blocks),
        in_specs=[VMEM_SPEC] * count,
        out_specs=(VMEM_SPEC,) * count,
        scratch_shapes=[
            pltpu.SemaphoreType.DMA((count,)),
            pltpu.SemaphoreType.DMA((count,)),
            pltpu.SemaphoreType.DMA((count,)),
        ],
        compiler_params=pltpu.CompilerParams(collective_id=collective_id, has_side_effects=True),
        name=name,
    )(*blocks)


def place_kernel(got_ref, meta_ref, low_ref, high_ref):
    n_dev, span, width = got_ref.shape
    total = n_dev * span
    half = low_ref.shape[0]
    coded = jnp.transpose(meta_ref[...])[:CAP].astype(I32)
    spread = onehot((iota((n_dev, total), 1) >> 4) == iota((n_dev, total), 0))
    high8 = (coded >> 8).astype(F32).astype(BF16)
    low8 = (coded & 255).astype(F32).astype(BF16)
    spreaded = dot_nn(high8, spread) * 256.0 + dot_nn(low8, spread)
    lane = iota((CAP, total), 1)
    row = jnp.sum(
        jnp.where((lane & (CAP - 1)) == iota((CAP, total), 0), spreaded, 0.0), axis=0, keepdims=True
    ).astype(I32) - 1
    is_grad = (iota((1, total), 1) & CAP) != 0
    row_p = jnp.where(is_grad, -1, row)
    row_g = jnp.where(is_grad, row, -1)
    got = got_ref[...].reshape(total, width)
    for index, out in enumerate((low_ref, high_ref)):
        ids = iota((half, total), 0) + index * half
        out[:, :width] = dot_nn(onehot(ids == row_p), got).astype(BF16)
        out[:, width:] = dot_nn(onehot(ids == row_g), got).astype(BF16)


def place(got, meta, half):
    width = got.shape[-1]
    shape = jax.ShapeDtypeStruct((half, 2 * width), BF16)
    return pl.pallas_call(
        place_kernel,
        out_shape=(shape, shape),
        in_specs=[VMEM_SPEC] * 2,
        out_specs=(VMEM_SPEC,) * 2,
        name="place",
    )(got, meta)


def patch_kernel(
    own_ref, next_ref, wqkv_ref, wout_ref, part_ref, igrad_own_ref, igrad_next_ref,
    x_s, g_s, q_s, k_s, v_s, ga_s, kt_s, vt_s, gat_s, attnt_s, gqkv_s,
):
    half, width2 = own_ref.shape
    width = width2 // 2
    rows = 2 * half
    x_s[:half] = own_ref[:, :width]
    x_s[half:] = next_ref[:, :width]
    g_s[:half] = own_ref[:, width:]
    g_s[half:] = next_ref[:, width:]
    pairs = width // 128
    scale = 1.0 / math.sqrt(width // HEADS)

    x = x_s[...]
    qkv = dot_nn(x, wqkv_ref[...])
    ga = dot_nt(g_s[...], wout_ref[...])
    for p in range(pairs):
        cols = slice(p * 128, (p + 1) * 128)
        q_s[p] = (qkv[:, cols].astype(BF16).astype(F32) * scale).astype(BF16)
        k = qkv[:, width + p * 128 : width + (p + 1) * 128].astype(BF16)
        v = qkv[:, 2 * width + p * 128 : 2 * width + (p + 1) * 128].astype(BF16)
        g = ga[:, cols].astype(BF16)
        k_s[p] = k
        v_s[p] = v
        ga_s[p] = g
        kt_s[p] = jnp.transpose(k)
        vt_s[p] = jnp.transpose(v)
        gat_s[p] = jnp.transpose(g)

    def body(p, carry):
        q = q_s[p]
        k = k_s[p]
        v = v_s[p]
        g = ga_s[p]
        grad_k = jnp.zeros((rows, 128), F32)
        grad_v = jnp.zeros((rows, 128), F32)
        lane = iota((rows, 128), 1) // 64
        grad_qt = []
        for h in range(2):
            part = slice(h * 64, (h + 1) * 64)
            keep = lane == h
            qh = jnp.where(keep, q.astype(F32), 0.0).astype(BF16)
            gh = jnp.where(keep, g.astype(F32), 0.0).astype(BF16)
            st = dot_nt(k, qh)
            top = jnp.max(st, axis=0, keepdims=True)
            e = jnp.exp(st - top)
            total = jnp.sum(e, axis=0, keepdims=True)
            pt = e * (1.0 / total)
            low = pt.astype(BF16)
            attnt = dot_nn(vt_s[p, part, :], low).astype(BF16)
            attnt_s[p, part, :] = attnt
            delta = jnp.sum(
                attnt.astype(F32) * gat_s[p, part, :].astype(F32), axis=0, keepdims=True
            )
            grad_v += dot_nn(low, gh)
            gpt = dot_nt(v, gh)
            gst = (pt * (gpt - delta)).astype(BF16)
            grad_k += dot_nn(gst, qh)
            grad_qt.append(dot_nn(kt_s[p, part, :], gst))
        gq = jnp.transpose(jnp.concatenate(grad_qt, axis=0) * scale)
        gqkv_s[p] = gq.astype(BF16)
        gqkv_s[pairs + p] = grad_k.astype(BF16)
        gqkv_s[2 * pairs + p] = grad_v.astype(BF16)
        return carry

    lax.fori_loop(0, pairs, body, 0)
    xt = jnp.transpose(x_s[...])
    igrad = jnp.zeros((rows, width), F32)
    for block in range(3 * pairs // 2):
        gq = jnp.concatenate([gqkv_s[2 * block], gqkv_s[2 * block + 1]], axis=1)
        part_ref[block] = dot_nn(xt, gq).astype(BF16)
        igrad += dot_nt(gq, wqkv_ref[:, block * 256 : (block + 1) * 256])
    igrad = igrad.astype(BF16)
    igrad_own_ref[...] = igrad[:half]
    igrad_next_ref[...] = igrad[half:]
    attnt = attnt_s[...].reshape(width, rows)
    pout = dot_nn(attnt, g_s[...])
    for block in range(width // 256):
        part_ref[3 * pairs // 2 + block] = pout[:, block * 256 : (block + 1) * 256].astype(BF16)


def patch_backward(own, following, w_qkv, w_out):
    half, width2 = own.shape
    width = width2 // 2
    rows = 2 * half
    pairs = width // 128
    tall = pltpu.VMEM((pairs, rows, 128), BF16)
    wide = pltpu.VMEM((pairs, 128, rows), BF16)
    return pl.pallas_call(
        patch_kernel,
        out_shape=(
            jax.ShapeDtypeStruct((4 * width // 256, width, 256), BF16),
            jax.ShapeDtypeStruct((half, width), BF16),
            jax.ShapeDtypeStruct((half, width), BF16),
        ),
        in_specs=[VMEM_SPEC] * 4,
        out_specs=(VMEM_SPEC,) * 3,
        scratch_shapes=[
            pltpu.VMEM((rows, width), BF16),
            pltpu.VMEM((rows, width), BF16),
            tall, tall, tall, tall, wide, wide, wide, wide,
            pltpu.VMEM((3 * pairs, rows, 128), BF16),
        ],
        name="patch",
    )(own, following, w_qkv, w_out)


def pick_kernel(low_ref, high_ref, meta_ref, send_ref):
    n_dev, span, width = send_ref.shape
    half = low_ref.shape[0]
    total = n_dev * span
    coded = meta_ref[...].astype(I32)
    spread = onehot((iota((total, n_dev), 0) >> 3) == iota((total, n_dev), 1))
    high = (coded >> 8).astype(F32).astype(BF16)
    low = (coded & 255).astype(F32).astype(BF16)
    spreaded = dot_nn(spread, high) * 256.0 + dot_nn(spread, low)
    own = iota((total, 128), 1) == (iota((total, 128), 0) & (CAP - 1))
    row = jnp.sum(jnp.where(own, spreaded, 0.0), axis=1, keepdims=True).astype(I32) - 1
    lane = iota((total, half), 1)
    block = dot_nn(onehot(lane == row), low_ref[...]) + dot_nn(
        onehot(lane + half == row), high_ref[...]
    )
    send_ref[...] = block.reshape(n_dev, span, width).astype(BF16)


def pick(low, high, meta):
    n_dev = meta.shape[0]
    return pl.pallas_call(
        pick_kernel,
        out_shape=jax.ShapeDtypeStruct((n_dev, CAP, low.shape[1]), BF16),
        in_specs=[VMEM_SPEC] * 3,
        out_specs=VMEM_SPEC,
        name="pick",
    )(low, high, meta)


def collect_kernel(got_ref, slot_ref, out_ref):
    n_dev, span, width = got_ref.shape
    rows = out_ref.shape[0]
    total = n_dev * span
    slot = jnp.transpose(jnp.broadcast_to(slot_ref[...].astype(F32), (128, rows)))[:, :1]
    hot = onehot(iota((rows, total), 1) == slot.astype(I32))
    got = got_ref[...].astype(F32).reshape(total, width).astype(BF16)
    out_ref[...] = dot_nn(hot, got).astype(BF16)


def collect(got, slot):
    rows = slot.shape[1]
    return pl.pallas_call(
        collect_kernel,
        out_shape=jax.ShapeDtypeStruct((rows, got.shape[2]), BF16),
        in_specs=[VMEM_SPEC] * 2,
        out_specs=VMEM_SPEC,
        name="collect",
    )(got, slot)


def reduce_kernel(
    part_ref, out_ref, r0, b0, r1, b1, r2, a3, a4, send_sem, recv_sem
):
    c = lax.axis_index("curve")
    d = lax.axis_index("dp")
    core = lax.rem(c, 2)
    x = lax.rem(c // 2, 4)
    z = lax.rem(c // 8, 8)
    y = d * 2 + c // 64
    plane = y * 4 + x
    barrier = pltpu.get_barrier_semaphore()

    def place_of(plane_id, z_id, core_id):
        yy = plane_id // 4
        xx = lax.rem(plane_id, 4)
        curve = ((lax.rem(yy, 2) * 8 + z_id) * 4 + xx) * 2 + core_id
        return {"curve": curve, "dp": yy // 2}

    def plane_peer(k):
        return lax.rem(plane + k, 16)

    def z_peer(k):
        return lax.rem(z + k, 8)

    partner = place_of(plane, z, 1 - core)

    def signal(device):
        pl.semaphore_signal(barrier, inc=1, device_id=device, device_id_type=MESH)

    signal(partner)

    def greet_plane(k, carry):
        signal(place_of(plane_peer(k), z, core))
        return carry

    def greet_z(k, carry):
        signal(place_of(plane, z_peer(k), core))
        return carry

    lax.fori_loop(1, 16, greet_plane, 0)
    lax.fori_loop(1, 8, greet_z, 0)
    pl.semaphore_wait(barrier, 23)

    def copy_to(src, dst, stage, device):
        return pltpu.make_async_remote_copy(
            src_ref=src, dst_ref=dst, send_sem=send_sem.at[stage], recv_sem=recv_sem.at[stage],
            device_id=device, device_id_type=MESH,
        )

    def wait_all(ref, count, stage):
        part = ref.at[pl.ds(0, count)]
        pltpu.make_async_copy(part, part, send_sem.at[stage]).wait()
        pltpu.make_async_copy(part, part, recv_sem.at[stage]).wait()

    first = copy_to(part_ref.at[1 - core], r0, 0, partner)
    first.start()
    first.wait()

    def add_first(i, carry):
        b0[i] = (part_ref[core, i].astype(F32) + r0[i].astype(F32)).astype(BF16)
        return carry

    lax.fori_loop(0, 16, add_first, 0)

    def send_plane(k, carry):
        peer = plane_peer(k)
        copy_to(b0.at[peer], r1.at[plane], 1, place_of(peer, z, core)).start()
        return carry

    lax.fori_loop(1, 16, send_plane, 0)
    r1[plane] = b0[plane]
    wait_all(r1, 15, 1)

    def add_plane(i, total):
        return total + r1[i].astype(F32)

    total = lax.fori_loop(0, 16, add_plane, jnp.zeros((128, 256), F32))
    b1[...] = total.astype(BF16).reshape(8, 16, 256)

    def send_z(k, carry):
        peer = z_peer(k)
        copy_to(b1.at[peer], r2.at[z], 2, place_of(plane, peer, core)).start()
        return carry

    lax.fori_loop(1, 8, send_z, 0)
    r2[z] = b1[z]
    wait_all(r2, 7, 2)
    final = jnp.sum(r2[...].astype(F32), axis=0)
    a3[z] = final.astype(BF16)

    def back_z(k, carry):
        copy_to(a3.at[z], a3.at[z], 3, place_of(plane, z_peer(k), core)).start()
        return carry

    lax.fori_loop(1, 8, back_z, 0)
    wait_all(a3, 7, 3)
    a4[plane] = a3[...].reshape(128, 256)

    def back_plane(k, carry):
        copy_to(a4.at[plane], a4.at[plane], 4, place_of(plane_peer(k), z, core)).start()
        return carry

    lax.fori_loop(1, 16, back_plane, 0)
    wait_all(a4, 15, 4)
    last = copy_to(a4, out_ref.at[core], 5, partner)
    last.start()
    out_ref[core] = a4[...]
    last.wait()


def reduce_parts(part):
    block = pltpu.VMEM((16, 128, 256), BF16)
    small = pltpu.VMEM((8, 16, 256), BF16)
    return pl.pallas_call(
        reduce_kernel,
        out_shape=jax.ShapeDtypeStruct(part.shape, BF16),
        in_specs=[VMEM_SPEC],
        out_specs=VMEM_SPEC,
        scratch_shapes=[
            block, block, block, small, small, small, block,
            pltpu.SemaphoreType.DMA((6,)),
            pltpu.SemaphoreType.DMA((6,)),
        ],
        compiler_params=pltpu.CompilerParams(collective_id=2, has_side_effects=True),
        name="reduce",
    )(part)


def on_device(points, grad_out, dest_dev, dest_row, w_qkv, w_out):
    n_dev = lax.axis_size("curve")
    rows, width = points.shape[1:]
    half = PATCH // 2
    to_previous = [(i, (i - 1) % n_dev) for i in range(n_dev)]
    to_next = [(i, (i + 1) % n_dev) for i in range(n_dev)]
    send, meta, slot = pack(dest_dev, dest_row, points[0], grad_out[0], n_dev)
    got, got_meta = exchange((send, meta.reshape(n_dev, 1, 128)), 0, "dispatch")
    got_meta = got_meta.reshape(n_dev, 128)
    low, high = place(got, got_meta, half)
    following = lax.ppermute(low, "curve", to_previous)
    part, igrad_own, igrad_next = patch_backward(high, following, w_qkv, w_out)
    igrad_low = lax.ppermute(igrad_next, "curve", to_next)
    back = pick(igrad_low, igrad_own, got_meta)
    (returned,) = exchange((back,), 1, "giveback")
    result = collect(returned, slot)
    summed = reduce_parts(part.reshape(2, 16, 128, 256)).reshape(4 * width // 256, width, 256)
    weights = jnp.transpose(summed, (1, 0, 2)).reshape(width, 4 * width).astype(F32)
    return (result[None], weights[:, : 3 * width], weights[:, 3 * width :])


def solution(mesh):
    placed = (
        P("dp", "curve", None),
        P("dp", "curve", None),
        P("dp", "curve"),
        P("dp", "curve"),
        P(),
        P(),
    )
    return jax.shard_map(
        on_device,
        mesh=mesh,
        in_specs=placed,
        out_specs=(P("dp", "curve", None), P(), P()),
        check_vma=False,
    )
```

profile of v0, /device:TPU:1, one launch (start us, length us, event | category | flops | bytes accessed | tf_op | source)
XLA Modules:
  0.0 203.8 jit_solution(232486184904044569)
XLA Ops:
  0.6 6.6 %pack.1 = (bf16[128,16,512]{2,1,0:T(8,128)(2,1)}, f32[128,128]{1,0:T(8,128)}, s32[1,512]{1,0:T(1,128)}) custom-call(s32[1,512]{1,0:T(1,128)} %dev_ref.1, s32[1,512]{1,0:T(1,128)} %row_ref.1, bf16[512,512]{1,0:T(8,128)(2,1)} %bitcast.16, bf16[512,512]{1,0:T(8,128)(2,1)} %bitcast.17), custom_call_target="tpu_custom_call" | custom-call | tf_op jit(solution)/shard_map/pack/pallas_call | solution.py:70
  7.2 62.6 %dispatch.1 = (bf16[128,16,512]{2,1,0:T(8,128)(2,1)}, f32[128,1,128]{2,1,0:T(1,128)}) custom-call(bf16[128,16,512]{2,1,0:T(8,128)(2,1)} %get-tuple-element.13.refs_0_, f32[128,1,128]{2,1,0:T(1,128)} %bitcast.21), custom_call_target="tpu_custom_call" | custom-call | tf_op jit(solution)/shard_map/dispatch/pallas_call | solution.py:128
  69.9 5.0 %place.1 = (bf16[256,1024]{1,0:T(8,128)(2,1)}, bf16[256,1024]{1,0:T(8,128)(2,1)}) custom-call(bf16[128,16,512]{2,1,0:T(8,128)(2,1)} %get-tuple-element.15.got_ref, f32[128,128]{1,0:T(8,128)} %bitcast.19), custom_call_target="tpu_custom_call" | custom-call | tf_op jit(solution)/shard_map/place/pallas_call | solution.py:169
  74.9 0.4 collective-permute-start
  75.3 8.4 %collective-permute-done.next_ref = bf16[256,1024]{1,0:T(8,128)(2,1)S(1)} collective-permute-done((bf16[256,1024]{1,0:T(8,128)(2,1)}, bf16[256,1024]{1,0:T(8,128)(2,1)S(1)}, u32[]{:S(2)}, u32[]{:S(2)}) %collective-permute-start) | collective-permute-done | bytes 524320 | tf_op jit(solution)/shard_map/ppermute | solution.py:474
  83.7 0.0 copy-start
  83.7 0.8 copy-done
  84.5 16.6 %patch.1 = (bf16[8,512,256]{2,1,0:T(8,128)(2,1)}, bf16[256,512]{1,0:T(8,128)(2,1)}, bf16[256,512]{1,0:T(8,128)(2,1)}) custom-call(bf16[256,1024]{1,0:T(8,128)(2,1)} %get-tuple-element.17.own_ref, bf16[256,1024]{1,0:T(8,128)(2,1)} %copy-done, bf16[512,1536]{1,0:T(8,128)(2,1)} %wqkv_ref.1, bf16[512,512]{1,0:T(8,128)(2,1)} %wout_ref.1), custom_call_target="tpu_custom_call" | custom-call | tf_op jit(solution)/shard_map/patch/pallas_call | solution.py:267
  101.1 0.0 collective-permute-start.1
  101.1 57.5 %reduce.1 = bf16[2,16,128,256]{3,2,1,0:T(8,128)(2,1)} custom-call(bf16[2,16,128,256]{3,2,1,0:T(8,128)(2,1)} %bitcast.15), custom_call_target="tpu_custom_call" | custom-call | tf_op jit(solution)/shard_map/reduce/pallas_call | solution.py:449
  158.5 2.0 convert_bitcast_fusion
  160.5 0.6 copy.10
  161.1 1.1 slice.9
  162.2 2.0 slice.8
  164.1 0.0 collective-permute-done.1.low_ref
  164.1 0.0 copy-start.1
  164.1 0.7 copy-done.1
  164.8 2.9 %pick.1.refs_0_ = bf16[128,8,512]{2,1,0:T(8,128)(2,1)} custom-call(bf16[256,512]{1,0:T(8,128)(2,1)} %copy-done.1, bf16[256,512]{1,0:T(8,128)(2,1)} %get-tuple-element.20.high_ref, f32[128,128]{1,0:T(8,128)} %bitcast.20), custom_call_target="tpu_custom_call" | custom-call | tf_op jit(solution)/shard_map/pick/pallas_call | solution.py:306
  167.8 32.9 %giveback.1.got_ref = bf16[128,8,512]{2,1,0:T(8,128)(2,1)} custom-call(bf16[128,8,512]{2,1,0:T(8,128)(2,1)} %pick.1.refs_0_), custom_call_target="tpu_custom_call" | custom-call | tf_op jit(solution)/shard_map/giveback/pallas_call | solution.py:128
  200.7 3.0 %collect.1 = bf16[512,512]{1,0:T(8,128)(2,1)} custom-call(bf16[128,8,512]{2,1,0:T(8,128)(2,1)} %giveback.1.got_ref, s32[1,512]{1,0:T(1,128)} %get-tuple-element.21.slot_ref), custom_call_target="tpu_custom_call" | custom-call | tf_op jit(solution)/shard_map/collect/pallas_call | solution.py:327
Async XLA Ops:
  74.9 8.8 %collective-permute-start = (bf16[256,1024]{1,0:T(8,128)(2,1)}, bf16[256,1024]{1,0:T(8,128)(2,1)S(1)}, u32[]{:S(2)}, u32[]{:S(2)}) collective-permute-start(bf16[256,1024]{1,0:T(8,128)(2,1)} %get-tuple-element.18), channel_id=1, source_target_pairs={{0,254},{2,0},{4,2},{6,4},{8,6},{10,8},{12,10},{14,12},{16,14},{18... | collective-permute-start | bytes 1572872 | tf_op jit(solution)/shard_map/ppermute | solution.py:474
  83.7 0.8 copy-start
  101.1 63.1 %collective-permute-start.1 = (bf16[256,512]{1,0:T(8,128)(2,1)}, bf16[256,512]{1,0:T(8,128)(2,1)S(1)}, u32[]{:S(2)}, u32[]{:S(2)}) collective-permute-start(bf16[256,512]{1,0:T(8,128)(2,1)} %get-tuple-element.19), channel_id=1, source_target_pairs={{0,2},{2,4},{4,6},{6,8},{8,10},{10,12},{12,14},{14,16},{16,18},{18... | collective-permute-start | bytes 786440 | tf_op jit(solution)/shard_map/ppermute | solution.py:476
  164.1 0.7 copy-start.1
where the time goes:
time: 204 us
  Pallas kernels  187 us (92%)
  waiting for transfers between devices  8.41 us (4%)
  local copies, waits for them, and re-layouts  5.13 us (3%)
    pallas_call x2, Pallas kernels, exchange(): pl.pallas_call(functools.partial(exchange_kernel, count), out_shape=tuple...  95.5 us
    pallas_call x1, Pallas kernels, reduce_parts(): pl.pallas_call(reduce_kernel, out_shape=jax.ShapeDtypeStruct(part.shape,...  57.5 us
    pallas_call x1, Pallas kernels, patch_backward(): pl.pallas_call(patch_kernel, out_shape=(jax.ShapeDtypeStruct((4 * width /...  16.6 us
    ppermute x1, waiting for transfers between devices, on_device(): following = lax.ppermute(low, 'curve', to_previous)  8.41 us
    pallas_call x1, Pallas kernels, pack(): pl.pallas_call(pack_kernel, out_shape=(jax.ShapeDtypeStruct((n_dev, 2 * C...  6.61 us
    pallas_call x1, Pallas kernels, place(): pl.pallas_call(place_kernel, out_shape=(shape, shape), in_specs=[VMEM_SPE...  5.01 us
  transfers between devices with their start and end apart: 2, of which 1 were waited for; matrix products, arithmetic and copies ran while one was open for 3% of the time, Pallas kernels for 28%

commit v1 on v0

v1 whole, which is shorter than its diff:
```python
import functools
import math

import jax
import jax.numpy as jnp
from jax import lax
from jax.experimental import pallas as pl
from jax.experimental.pallas import tpu as pltpu
from jax.sharding import PartitionSpec as P

HEADS = 8
PATCH = 512
CAP = 8
MESH = pl.DeviceIdType.MESH
BF16 = jnp.bfloat16
F32 = jnp.float32
I32 = jnp.int32
VMEM_SPEC = pl.BlockSpec(memory_space=pltpu.VMEM)
ANY_SPEC = pl.BlockSpec(memory_space=pl.ANY)


def dot_nn(a, b):
    return lax.dot_general(a, b, (((1,), (0,)), ((), ())), preferred_element_type=F32)


def dot_nt(a, b):
    return lax.dot_general(a, b, (((1,), (1,)), ((), ())), preferred_element_type=F32)


def iota(shape, dim):
    return lax.broadcasted_iota(I32, shape, dim)


def onehot(mask):
    return jnp.where(mask, 1.0, 0.0).astype(BF16)


def signal(barrier, device):
    pl.semaphore_signal(barrier, inc=1, device_id=device, device_id_type=MESH)


def greet_curve(barrier, me, n_dev):
    def greet(k, carry):
        signal(barrier, {"curve": lax.rem(me + k, n_dev)})
        return carry

    lax.fori_loop(1, n_dev, greet, 0)


def remote(src, dst, send_sem, recv_sem, device):
    return pltpu.make_async_remote_copy(
        src_ref=src, dst_ref=dst, send_sem=send_sem, recv_sem=recv_sem,
        device_id=device, device_id_type=MESH,
    )


def wait_bytes(ref, sem):
    pltpu.make_async_copy(ref, ref, sem).wait()


CHUNK = 16


def send_chunk(send, got, send_sem, recv_sem, me, group, n_dev):
    def one(k, carry):
        peer = group * CHUNK + k

        @pl.when(peer != me)
        def _():
            remote(send.at[peer], got.at[me], send_sem, recv_sem, {"curve": peer}).start()

        return carry

    lax.fori_loop(0, CHUNK, one, 0)

def front_kernel(
    dev_ref, row_ref, points_ref, grads_ref, x_ref, g_ref, gotm_ref, slot_ref,
    send_p, send_g, send_m, got_p, got_g, got_m, low_p, low_g, sems,
):
    n_dev, span, width = send_p.shape
    rows = points_ref.shape[0]
    half = rows // 2
    groups = n_dev // CHUNK
    me = lax.axis_index("curve")
    previous = {"curve": lax.rem(me + n_dev - 1, n_dev)}
    barrier = pltpu.get_barrier_semaphore()
    greet_curve(barrier, me, n_dev)

    dev = dev_ref[...]
    mask = iota((n_dev, rows), 0) == dev
    hot = onehot(mask)
    upper = onehot(iota((rows, rows), 0) <= iota((rows, rows), 1))
    running = dot_nn(hot, upper)
    rank = jnp.sum(jnp.where(mask, running, 0.0), axis=0, keepdims=True).astype(I32) - 1
    slot = dev * CAP + rank
    slot_ref[...] = slot

    def make(group):
        ids = iota((CHUNK * CAP, rows), 0) + group * (CHUNK * CAP)
        pick = onehot(ids == slot)
        where = pl.ds(group * CHUNK, CHUNK)
        send_p[where] = dot_nn(pick, points_ref[...]).reshape(CHUNK, CAP, width).astype(BF16)
        send_g[where] = dot_nn(pick, grads_ref[...]).reshape(CHUNK, CAP, width).astype(BF16)

    home = me // CHUNK
    make(home)
    pl.semaphore_wait(barrier, n_dev - 1)

    def step(s, carry):
        make(lax.rem(home + s, groups))
        send_chunk(
            send_p, got_p, sems.at[0, 0], sems.at[1, 0], me, lax.rem(home + s - 1, groups), n_dev
        )
        return carry

    lax.fori_loop(1, groups, step, 0)
    coded = row_ref[...] + 1
    at_rank = iota((128, rows), 0) == rank
    high = jnp.where(at_rank, (coded >> 8).astype(F32), 0.0).astype(BF16)
    low = jnp.where(at_rank, (coded & 255).astype(F32), 0.0).astype(BF16)
    meta = dot_nt(hot, high) * 256.0 + dot_nt(hot, low)
    send_m[...] = meta.reshape(n_dev, 1, 128)
    send_chunk(
        send_p, got_p, sems.at[0, 0], sems.at[1, 0], me, lax.rem(home + groups - 1, groups), n_dev
    )

    def rest(s, carry):
        group = lax.rem(home + s, groups)
        send_chunk(send_m, got_m, sems.at[0, 1], sems.at[1, 1], me, group, n_dev)
        return carry

    def grads(s, carry):
        group = lax.rem(home + s, groups)
        send_chunk(send_g, got_g, sems.at[0, 2], sems.at[1, 2], me, group, n_dev)
        return carry

    lax.fori_loop(0, groups, rest, 0)
    lax.fori_loop(0, groups, grads, 0)
    got_p[me] = send_p[me]
    got_m[me] = send_m[me]
    got_g[me] = send_g[me]

    others = pl.ds(0, n_dev - 1)
    wait_bytes(got_m.at[others], sems.at[1, 1])
    meta = got_m[...].reshape(n_dev, 128)
    gotm_ref[...] = meta
    total = n_dev * span
    coded = jnp.transpose(meta)[:CAP].astype(I32)
    spread = onehot((iota((n_dev, total), 1) >> 3) == iota((n_dev, total), 0))
    high8 = (coded >> 8).astype(F32).astype(BF16)
    low8 = (coded & 255).astype(F32).astype(BF16)
    spreaded = dot_nn(high8, spread) * 256.0 + dot_nn(low8, spread)
    lane = iota((CAP, total), 1)
    row = jnp.sum(
        jnp.where((lane & (CAP - 1)) == iota((CAP, total), 0), spreaded, 0.0), axis=0, keepdims=True
    ).astype(I32) - 1
    place_low = onehot(iota((half, total), 0) == row)
    place_high = onehot(iota((half, total), 0) + half == row)
    parts = ((0, got_p, low_p, x_ref), (2, got_g, low_g, g_ref))
    for index, got_ref, low_ref, out_ref in parts:
        wait_bytes(got_ref.at[others], sems.at[1, index])
        got = got_ref[...].astype(F32).reshape(total, width).astype(BF16)
        low_ref[...] = dot_nn(place_low, got).astype(BF16)
        out_ref[pl.ds(0, half)] = dot_nn(place_high, got).astype(BF16)
        remote(
            low_ref, out_ref.at[pl.ds(half, half)], sems.at[0, 3 + index], sems.at[1, 3 + index],
            previous,
        ).start()
    wait_bytes(send_p.at[others], sems.at[0, 0])
    wait_bytes(send_m.at[others], sems.at[0, 1])
    wait_bytes(send_g.at[others], sems.at[0, 2])
    for index, got_ref, low_ref, out_ref in parts:
        wait_bytes(low_ref, sems.at[0, 3 + index])
        wait_bytes(out_ref.at[pl.ds(half, half)], sems.at[1, 3 + index])


def front(dev, row, points, grads, n_dev):
    rows, width = points.shape
    whole = jax.ShapeDtypeStruct((rows, width), BF16)
    slots = pltpu.VMEM((n_dev, CAP, width), BF16)
    metas = pltpu.VMEM((n_dev, 1, 128), F32)
    lows = pltpu.VMEM((rows // 2, width), BF16)
    return pl.pallas_call(
        front_kernel,
        out_shape=(
            whole,
            whole,
            jax.ShapeDtypeStruct((n_dev, 128), F32),
            jax.ShapeDtypeStruct((1, rows), I32),
        ),
        in_specs=[VMEM_SPEC] * 4,
        out_specs=(VMEM_SPEC,) * 4,
        scratch_shapes=[
            slots, slots, metas, slots, slots, metas, lows, lows,
            pltpu.SemaphoreType.DMA((2, 6)),
        ],
        compiler_params=pltpu.CompilerParams(collective_id=0, has_side_effects=True),
        name="front",
    )(dev, row, points, grads)


def patch_kernel(
    x_s, g_s, wqkv_ref, wout_ref, part_ref, igrad_own_ref, igrad_next_ref,
    q_s, k_s, v_s, ga_s, kt_s, vt_s, gat_s, attnt_s, gqkv_s,
):
    rows, width = x_s.shape
    half = rows // 2
    pairs = width // 128
    scale = 1.0 / math.sqrt(width // HEADS)

    x = x_s[...]
    qkv = dot_nn(x, wqkv_ref[...])
    ga = dot_nt(g_s[...], wout_ref[...])
    for p in range(pairs):
        cols = slice(p * 128, (p + 1) * 128)
        q_s[p] = (qkv[:, cols].astype(BF16).astype(F32) * scale).astype(BF16)
        k = qkv[:, width + p * 128 : width + (p + 1) * 128].astype(BF16)
        v = qkv[:, 2 * width + p * 128 : 2 * width + (p + 1) * 128].astype(BF16)
        g = ga[:, cols].astype(BF16)
        k_s[p] = k
        v_s[p] = v
        ga_s[p] = g
        kt_s[p] = jnp.transpose(k)
        vt_s[p] = jnp.transpose(v)
        gat_s[p] = jnp.transpose(g)

    def body(p, carry):
        q = q_s[p]
        k = k_s[p]
        v = v_s[p]
        g = ga_s[p]
        grad_k = jnp.zeros((rows, 128), F32)
        grad_v = jnp.zeros((rows, 128), F32)
        lane = iota((rows, 128), 1) // 64
        grad_qt = []
        for h in range(2):
            part = slice(h * 64, (h + 1) * 64)
            keep = lane == h
            qh = jnp.where(keep, q.astype(F32), 0.0).astype(BF16)
            gh = jnp.where(keep, g.astype(F32), 0.0).astype(BF16)
            st = dot_nt(k, qh)
            top = jnp.max(st, axis=0, keepdims=True)
            e = jnp.exp(st - top)
            total = jnp.sum(e, axis=0, keepdims=True)
            pt = e * (1.0 / total)
            low = pt.astype(BF16)
            attnt = dot_nn(vt_s[p, part, :], low).astype(BF16)
            attnt_s[p, part, :] = attnt
            delta = jnp.sum(
                attnt.astype(F32) * gat_s[p, part, :].astype(F32), axis=0, keepdims=True
            )
            grad_v += dot_nn(low, gh)
            gpt = dot_nt(v, gh)
            gst = (pt * (gpt - delta)).astype(BF16)
            grad_k += dot_nn(gst, qh)
            grad_qt.append(dot_nn(kt_s[p, part, :], gst))
        gq = jnp.transpose(jnp.concatenate(grad_qt, axis=0) * scale)
        gqkv_s[p] = gq.astype(BF16)
        gqkv_s[pairs + p] = grad_k.astype(BF16)
        gqkv_s[2 * pairs + p] = grad_v.astype(BF16)
        return carry

    lax.fori_loop(0, pairs, body, 0)
    xt = jnp.transpose(x_s[...])
    igrad = jnp.zeros((rows, width), F32)
    for block in range(3 * pairs // 2):
        gq = jnp.concatenate([gqkv_s[2 * block], gqkv_s[2 * block + 1]], axis=1)
        part = dot_nn(xt, gq).astype(BF16)
        part_ref[2 * block] = part[:, :128]
        part_ref[2 * block + 1] = part[:, 128:]
        igrad += dot_nt(gq, wqkv_ref[:, block * 256 : (block + 1) * 256])
    igrad = igrad.astype(BF16)
    igrad_own_ref[...] = igrad[:half]
    igrad_next_ref[...] = igrad[half:]
    attnt = attnt_s[...].reshape(width, rows)
    pout = dot_nn(attnt, g_s[...])
    for block in range(pairs):
        part_ref[3 * pairs + block] = pout[:, block * 128 : (block + 1) * 128].astype(BF16)


def patch_backward(x, g, w_qkv, w_out):
    rows, width = x.shape
    half = rows // 2
    pairs = width // 128
    tall = pltpu.VMEM((pairs, rows, 128), BF16)
    wide = pltpu.VMEM((pairs, 128, rows), BF16)
    return pl.pallas_call(
        patch_kernel,
        out_shape=(
            jax.ShapeDtypeStruct((4 * width // 128, width, 128), BF16),
            jax.ShapeDtypeStruct((half, width), BF16),
            jax.ShapeDtypeStruct((half, width), BF16),
        ),
        in_specs=[VMEM_SPEC] * 4,
        out_specs=(VMEM_SPEC,) * 3,
        scratch_shapes=[
            tall, tall, tall, tall, wide, wide, wide, wide,
            pltpu.VMEM((3 * pairs, rows, 128), BF16),
        ],
        name="patch",
    )(x, g, w_qkv, w_out)


def back_kernel(
    own_ref, next_ref, meta_ref, part_ref, got_ref, out_ref,
    low_s, send_s, r0, b0, r1, b1, r2, b2, r3, a3, a4, a5, back_sem, low_sem, send_sem, recv_sem,
):
    n_dev, span, width = send_s.shape
    half = own_ref.shape[0]
    groups = n_dev // CHUNK
    c = lax.axis_index("curve")
    d = lax.axis_index("dp")
    core = lax.rem(c, 2)
    x = lax.rem(c // 2, 4)
    z = lax.rem(c // 8, 8)
    y = d * 2 + c // 64
    barrier = pltpu.get_barrier_semaphore()

    def at(y_id, z_id, x_id, core_id):
        return {"curve": ((lax.rem(y_id, 2) * 8 + z_id) * 4 + x_id) * 2 + core_id, "dp": y_id // 2}

    def x_at(k):
        return lax.rem(x + k, 4)

    def y_at(k):
        return lax.rem(y + k, 4)

    def z_at(k):
        return lax.rem(z + k, 8)

    greet_curve(barrier, c, n_dev)
    for y_hat in range(2):
        signal(barrier, {"curve": lax.rem(c, 64) + 64 * y_hat, "dp": 1 - d})
    pl.semaphore_wait(barrier, n_dev + 1)

    def go(src, dst, stage, device):
        remote(src, dst, send_sem.at[stage], recv_sem.at[stage], device).start()

    def done(ref, stage):
        wait_bytes(ref, send_sem.at[stage])
        wait_bytes(ref, recv_sem.at[stage])

    def to_x(src, dst, stage):
        for k in range(1, 4):
            go(src(x_at(k)), dst, stage, at(y, z, x_at(k), core))

    def to_y(src, dst, stage):
        for k in range(1, 4):
            go(src(y_at(k)), dst, stage, at(y_at(k), z, x, core))

    partner = at(y, z, x, 1 - core)
    following = {"curve": lax.rem(c + 1, n_dev)}
    hand = remote(next_ref, low_s, low_sem.at[0], low_sem.at[1], following)
    hand.start()
    go(part_ref.at[1 - core], r0, 0, partner)
    hand.wait()

    def give(s):
        group = lax.rem(c // CHUNK + s, groups)
        coded = meta_ref[...].astype(I32)
        total = CHUNK * span
        spread = onehot(
            (iota((total, n_dev), 0) >> 3) + group * CHUNK == iota((total, n_dev), 1)
        )
        high = (coded >> 8).astype(F32).astype(BF16)
        low = (coded & 255).astype(F32).astype(BF16)
        spreaded = dot_nn(spread, high) * 256.0 + dot_nn(spread, low)
        mine = iota((total, 128), 1) == (iota((total, 128), 0) & (CAP - 1))
        row = jnp.sum(jnp.where(mine, spreaded, 0.0), axis=1, keepdims=True).astype(I32) - 1
        lane = iota((total, half), 1)
        block = dot_nn(onehot(lane == row), low_s[...]) + dot_nn(
            onehot(lane + half == row), own_ref[...]
        )
        send_s[pl.ds(group * CHUNK, CHUNK)] = block.reshape(CHUNK, span, width).astype(BF16)

    def give_many(first, last):
        def one(s, carry):
            give(s)
            group = lax.rem(c // CHUNK + s, groups)
            send_chunk(send_s, got_ref, back_sem.at[0], back_sem.at[1], c, group, n_dev)
            return carry

        lax.fori_loop(first, last, one, 0)

    give_many(0, 1)
    done(r0, 0)

    def add_first(i, carry):
        for h in range(2):
            for j in range(4):
                total = part_ref[core, h, i, j].astype(F32) + r0[h, i, j].astype(F32)
                b0[h, i, j] = total.astype(BF16)
        return carry

    lax.fori_loop(0, 4, add_first, 0)
    r1[0, x] = b0[0, x]
    r1[1, y] = b0[1, y]
    to_x(lambda p: b0.at[0, p], r1.at[0, x], 1)
    to_y(lambda p: b0.at[1, p], r1.at[1, y], 2)
    give_many(1, 3)
    done(r1.at[0, pl.ds(0, 3)], 1)
    done(r1.at[1, pl.ds(0, 3)], 2)
    for h in range(2):
        for j in range(4):
            total = r1[h, 0, j].astype(F32)
            for i in range(1, 4):
                total += r1[h, i, j].astype(F32)
            b1[h, j] = total.astype(BF16)
    r2[0, y] = b1[0, y]
    r2[1, x] = b1[1, x]
    to_y(lambda p: b1.at[0, p], r2.at[0, y], 3)
    to_x(lambda p: b1.at[1, p], r2.at[1, x], 4)
    give_many(3, 5)
    done(r2.at[0, pl.ds(0, 3)], 3)
    done(r2.at[1, pl.ds(0, 3)], 4)
    for h in range(2):
        total = r2[h, 0].astype(F32)
        for i in range(1, 4):
            total += r2[h, i].astype(F32)
        b2[:, h] = total.reshape(8, 16, 128).astype(BF16)
    r3[z] = b2[z]
    for k in range(1, 8):
        go(b2.at[z_at(k)], r3.at[z], 5, at(y, z_at(k), x, core))
    give_many(5, groups)
    done(r3.at[pl.ds(0, 7)], 5)
    final = r3[0].astype(F32)
    for k in range(1, 8):
        final += r3[k].astype(F32)
    a3[z] = final.astype(BF16)
    for k in range(1, 8):
        go(a3.at[z], a3.at[z], 6, at(y, z_at(k), x, core))
    got_ref[c] = send_s[c]
    done(a3.at[pl.ds(0, 7)], 6)
    a4[0, y] = a3[:, 0].reshape(128, 128)
    a4[1, x] = a3[:, 1].reshape(128, 128)
    to_y(lambda p: a4.at[0, y], a4.at[0, y], 7)
    to_x(lambda p: a4.at[1, x], a4.at[1, x], 8)
    done(a4.at[0, pl.ds(0, 3)], 7)
    done(a4.at[1, pl.ds(0, 3)], 8)
    a5[0, x] = a4[0]
    a5[1, y] = a4[1]
    to_x(lambda p: a5.at[0, x], a5.at[0, x], 9)
    to_y(lambda p: a5.at[1, y], a5.at[1, y], 10)
    done(a5.at[0, pl.ds(0, 3)], 9)
    done(a5.at[1, pl.ds(0, 3)], 10)
    go(a5, out_ref.at[core], 11, partner)
    out_ref[core] = a5[...]
    others = pl.ds(0, n_dev - 1)
    wait_bytes(send_s.at[others], back_sem.at[0])
    wait_bytes(got_ref.at[others], back_sem.at[1])
    done(a5, 11)


def back(igrad_own, igrad_next, meta, part):
    n_dev = meta.shape[0]
    half, width = igrad_own.shape
    slots = (n_dev, CAP, width)
    big = pltpu.VMEM((2, 4, 4, 128, 128), BF16)
    mid = pltpu.VMEM((2, 4, 128, 128), BF16)
    small = pltpu.VMEM((8, 2, 16, 128), BF16)
    return pl.pallas_call(
        back_kernel,
        out_shape=(
            jax.ShapeDtypeStruct(slots, BF16),
            jax.ShapeDtypeStruct(part.shape, BF16),
        ),
        in_specs=[VMEM_SPEC] * 4,
        out_specs=(VMEM_SPEC,) * 2,
        scratch_shapes=[
            pltpu.VMEM((half, width), BF16),
            pltpu.VMEM(slots, BF16),
            big, big, big, mid, mid, small, small, small, mid, big,
            pltpu.SemaphoreType.DMA((2,)),
            pltpu.SemaphoreType.DMA((2,)),
            pltpu.SemaphoreType.DMA((12,)),
            pltpu.SemaphoreType.DMA((12,)),
        ],
        compiler_params=pltpu.CompilerParams(collective_id=1, has_side_effects=True),
        name="back",
    )(igrad_own, igrad_next, meta, part)


def finish_kernel(got_ref, slot_ref, sum_ref, out_ref, wqkv_ref, wout_ref):
    n_dev, span, width = got_ref.shape
    rows = out_ref.shape[0]
    total = n_dev * span
    slot = jnp.transpose(jnp.broadcast_to(slot_ref[...].astype(F32), (128, rows)))[:, :1]
    hot = onehot(iota((rows, total), 1) == slot.astype(I32))
    got = got_ref[...].astype(F32).reshape(total, width).astype(BF16)
    out_ref[...] = dot_nn(hot, got).astype(BF16)
    blocks = 3 * width // 128
    for block in range(blocks):
        wqkv_ref[:, block * 128 : (block + 1) * 128] = sum_ref[block].astype(F32)
    for block in range(width // 128):
        wout_ref[:, block * 128 : (block + 1) * 128] = sum_ref[blocks + block].astype(F32)


def finish(got, slot, summed):
    rows = slot.shape[1]
    width = got.shape[2]
    return pl.pallas_call(
        finish_kernel,
        out_shape=(
            jax.ShapeDtypeStruct((rows, width), BF16),
            jax.ShapeDtypeStruct((width, 3 * width), F32),
            jax.ShapeDtypeStruct((width, width), F32),
        ),
        in_specs=[VMEM_SPEC] * 3,
        out_specs=(VMEM_SPEC,) * 3,
        name="finish",
    )(got, slot, summed)


def on_device(points, grad_out, dest_dev, dest_row, w_qkv, w_out):
    n_dev = lax.axis_size("curve")
    width = points.shape[2]
    x, g, meta, slot = front(dest_dev, dest_row, points[0], grad_out[0], n_dev)
    part, igrad_own, igrad_next = patch_backward(x, g, w_qkv, w_out)
    got, summed = back(igrad_own, igrad_next, meta, part.reshape(2, 2, 4, 4, 128, 128))
    result, weight_qkv, weight_out = finish(got, slot, summed.reshape(4 * width // 128, width, 128))
    return (result[None], weight_qkv, weight_out)


def solution(mesh):
    placed = (
        P("dp", "curve", None),
        P("dp", "curve", None),
        P("dp", "curve"),
        P("dp", "curve"),
        P(),
        P(),
    )
    return jax.shard_map(
        on_device,
        mesh=mesh,
        in_specs=placed,
        out_specs=(P("dp", "curve", None), P(), P()),
        check_vma=False,
    )
```

time: 204 us -> 160 us (0.78)
  Pallas kernels: 187 us -> 159 us
  waiting for transfers between devices: 8.41 us -> 0 us
  local copies, waits for them, and re-layouts: 5.13 us -> 0 us
    pallas_call x7 -> x3, Pallas kernels: 171 us -> 142 us  [the longest x1 69.5 us: back(): pl.pallas_call(back_kernel, out_shape=(jax.ShapeDtypeStruct(slots, BF16),...]
    ppermute x2 -> x0, waiting for transfers between devices: 8.41 us -> none  [the longest x1 8.41 us: on_device(): following = lax.ppermute(low, 'curve', to_previous)]
    slice x2 -> x0, local copies, waits for them, and re-layouts: 3.03 us -> none  [on_device(): return (result[None], weights[:, :3 * width], weights[:, 3 * width:])]
  transfers between devices with their start and end apart: 2 -> 0, of which waited for: 1 -> 0; matrix products, arithmetic and copies ran while one was open for 3% -> 0% of each run, Pallas kernels for 28% -> 0%
where the time goes in v1:
time: 160 us
  Pallas kernels  159 us (99%)
    pallas_call x1, Pallas kernels, back(): pl.pallas_call(back_kernel, out_shape=(jax.ShapeDtypeStruct(slots, BF16),...  69.5 us
    pallas_call x1, Pallas kernels, front(): pl.pallas_call(front_kernel, out_shape=(whole, whole, jax.ShapeDtypeStruc...  67.6 us
    pallas_call x1, Pallas kernels, patch_backward(): pl.pallas_call(patch_kernel, out_shape=(jax.ShapeDtypeStruct((4 * width /...  16.5 us
    pallas_call x1, Pallas kernels, finish(): pl.pallas_call(finish_kernel, out_shape=(jax.ShapeDtypeStruct((rows, widt...  5.29 us

profile of v1, /device:TPU:1, one launch (start us, length us, event | category | flops | bytes accessed | tf_op | source)
XLA Modules:
  0.0 159.6 jit_solution(7875946026204288233)
XLA Ops:
  0.6 67.6 %front.1 = (bf16[512,512]{1,0:T(8,128)(2,1)}, bf16[512,512]{1,0:T(8,128)(2,1)}, f32[128,128]{1,0:T(8,128)}, s32[1,512]{1,0:T(1,128)}) custom-call(s32[1,512]{1,0:T(1,128)} %dev_ref.1, s32[1,512]{1,0:T(1,128)} %row_ref.1, bf16[512,512]{1,0:T(8,128)(2,1)} %bitcast.7, bf16[512,512]{1,0:T(8,128)(2,1)} %bitcast.8), custom_call_target="tpu_custom_call" | custom-call | tf_op jit(solution)/shard_map/front/pallas_call | solution.py:183
  68.2 16.5 %patch.1 = (bf16[16,512,128]{2,1,0:T(8,128)(2,1)}, bf16[256,512]{1,0:T(8,128)(2,1)}, bf16[256,512]{1,0:T(8,128)(2,1)}) custom-call(bf16[512,512]{1,0:T(8,128)(2,1)} %get-tuple-element.15.x_s, bf16[512,512]{1,0:T(8,128)(2,1)} %get-tuple-element.16.g_s, bf16[512,1536]{1,0:T(8,128)(2,1)} %wqkv_ref.1, bf16[512,512]{1,0:T(8,128)(2,1)} %wout_ref.1), custom_call_target="tpu_custom_call" | custom-call | tf_op jit(solution)/shard_map/patch/pallas_call | solution.py:287
  84.8 69.5 %back.1 = (bf16[128,8,512]{2,1,0:T(8,128)(2,1)}, bf16[2,2,4,4,128,128]{5,4,3,2,1,0:T(8,128)(2,1)}) custom-call(bf16[256,512]{1,0:T(8,128)(2,1)} %get-tuple-element.17.own_ref, bf16[256,512]{1,0:T(8,128)(2,1)} %get-tuple-element.18.next_ref, f32[128,128]{1,0:T(8,128)} %get-tuple-element.19.meta_ref, bf16[2,2,4,4,128,128]{5,4,3,2,1,0:T(8,128)(2,1)} %bitcast.6), custom_call_target="tpu_custom_call" | custom-call | tf_op jit(solution)/shard_map/back/pallas_call | solution.py:461
  154.3 5.3 %finish.1 = (bf16[512,512]{1,0:T(8,128)(2,1)}, f32[512,1536]{1,0:T(8,128)}, f32[512,512]{1,0:T(8,128)}) custom-call(bf16[128,8,512]{2,1,0:T(8,128)(2,1)} %get-tuple-element.21.got_ref, s32[1,512]{1,0:T(1,128)} %get-tuple-element.22.slot_ref, bf16[16,512,128]{2,1,0:T(8,128)(2,1)} %bitcast.5), custom_call_target="tpu_custom_call" | custom-call | tf_op jit(solution)/shard_map/finish/pallas_call | solution.py:501
